TPU v7x, 32 devices: a whole 2x2x4 slice. The times are simulated.
32 devices in a mesh: dp: 16 (over z, y, core), fsdp: 2 (over x).
Axes of the slice: x: 2, y: 2, z: 4, core: 2. Of those that a mesh axis runs over, the one named last changes fastest.
Arguments:
- text_states: bfloat16 [256, 128, 768], P(('dp', 'fsdp')), may hold values from -6 to 6
- image_states: bfloat16 [64, 36, 1024], P(('dp', 'fsdp')), may hold values from -6 to 6
- text_lengths: int32 [256], P(('dp', 'fsdp')), may hold values from 8 to 128, as said below
- region_mask: int32 [64, 36], P(('dp', 'fsdp')), may hold values from 0 to 1, as said below
- group_ids: int32 [256], P(('dp', 'fsdp')), may hold values from 0 to 63, as said below
- image_query: bfloat16 [1024, 1024], P('dp', 'fsdp'), may hold values from -0.1875 to 0.1875
- image_key: bfloat16 [1024, 1024], P('dp', 'fsdp'), may hold values from -0.1875 to 0.1875
- image_value: bfloat16 [1024, 1024], P('dp', 'fsdp'), may hold values from -0.1875 to 0.1875
- text_query: bfloat16 [768, 1024], P('dp', 'fsdp'), may hold values from -0.21875 to 0.21875
- text_key: bfloat16 [768, 1024], P('dp', 'fsdp'), may hold values from -0.21875 to 0.21875
- text_value: bfloat16 [768, 1024], P('dp', 'fsdp'), may hold values from -0.21875 to 0.21875
- image_output: bfloat16 [1024, 1024], P('dp', 'fsdp'), may hold values from -1.5 to 1.5
- text_output: bfloat16 [1024, 768], P('dp', 'fsdp'), may hold values from -0.75 to 0.75
- image_inner: bfloat16 [1024, 1024], P('dp', 'fsdp'), may hold values from -0.1875 to 0.1875
- image_outer: bfloat16 [1024, 1024], P('dp', 'fsdp'), may hold values from -0.1875 to 0.1875
- text_inner: bfloat16 [768, 3072], P('dp', 'fsdp'), may hold values from -0.21875 to 0.21875
- text_outer: bfloat16 [3072, 768], P('dp', 'fsdp'), may hold values from -0.109375 to 0.109375
- norm_params: float32 [4, 1792], P(None, ('dp', 'fsdp')), may hold values from -1.2 to 2, as said below
- cot_text: bfloat16 [256, 128, 768], P(('dp', 'fsdp')), may hold values from -6 to 6
- cot_image: bfloat16 [256, 36, 1024], P(('dp', 'fsdp')), may hold values from -6 to 6
Outputs:
- text_out: bfloat16 [256, 128, 768], P(('dp', 'fsdp'))
- image_out: bfloat16 [256, 36, 1024], P(('dp', 'fsdp'))
- text_grad: float32 [256, 128, 768], P(('dp', 'fsdp'))
- image_grad: float32 [64, 36, 1024], P(('dp', 'fsdp'))
- image_query_grad: float32 [1024, 1024], P('dp', 'fsdp')
- image_key_grad: float32 [1024, 1024], P('dp', 'fsdp')
- image_value_grad: float32 [1024, 1024], P('dp', 'fsdp')
- text_query_grad: float32 [768, 1024], P('dp', 'fsdp')
- text_key_grad: float32 [768, 1024], P('dp', 'fsdp')
- text_value_grad: float32 [768, 1024], P('dp', 'fsdp')
- image_output_grad: float32 [1024, 1024], P('dp', 'fsdp')
- text_output_grad: float32 [1024, 768], P('dp', 'fsdp')
- image_inner_grad: float32 [1024, 1024], P('dp', 'fsdp')
- image_outer_grad: float32 [1024, 1024], P('dp', 'fsdp')
- text_inner_grad: float32 [768, 3072], P('dp', 'fsdp')
- text_outer_grad: float32 [3072, 768], P('dp', 'fsdp')
- norm_grad: float32 [4, 1792], P(None, ('dp', 'fsdp'))
Inputs may be any that keep to these rules, and one draw needn't show every extreme that they name: `text_lengths`: one pair has exactly 128 tokens and one has 8. `region_mask`: each image's regions fill a leading run of its slots, of 9 to 36 regions; one image has 36, one has 9. `group_ids`: the pairs of each aligned block of 8 pairs name the 2 images of the same block index, each of them exactly four times. `norm_params`: rows 0 and 2 are gains between 0.5 and 2, rows 1 and 3 shifts.
All inputs are finite; a program needn't handle non-finite values.
Results may differ from a plain program's by a relative error of at most 0.019.
Values may be sent and summed in bfloat16 or wider, within the bound.
A program may use at most 192 MiB of HBM per device.

v0:
```python
import functools
import math

import jax
import jax.numpy as jnp
from jax import lax
from jax.experimental import pallas as pl
from jax.experimental.pallas import tpu as pltpu
from jax.sharding import PartitionSpec as P

HDIM = 128

norm_eps = 1e-12
masked_score = -1e30

MESH_IDS = pl.DeviceIdType.MESH
VMEM_LIMIT = 63 * 1024 * 1024
WHOLE = pl.BlockSpec(memory_space=pltpu.VMEM)
SCALARS = pl.BlockSpec(memory_space=pltpu.SMEM)
ANYWHERE = pl.BlockSpec(memory_space=pl.ANY)
CORE = ("d", 0)


def bits_of(size):
    count = size.bit_length() - 1
    assert 1 << count == size
    return count


def mesh_bits():
    return bits_of(lax.axis_size("dp")), bits_of(lax.axis_size("fsdp"))


def hop_orders(nd, nf):
    high = [("d", b) for b in range(nd - 1, 2, -1)]
    low = [("d", 2)]
    near = [("d", 1)]
    wide = [("f", b) for b in range(nf)]
    return (low + near + high + wide, high + wide + low + near)


def cut_pieces(shapes):
    pieces, waves, large = [], [], 0
    for m, (rows, cols) in enumerate(shapes):
        count = 4 if rows * cols > 40000 else 2
        if rows % (16 * count) == 0:
            each = rows // count
            cuts = [(k * each, each, 0, cols) for k in range(count)]
        elif cols % (128 * count) == 0 and rows % 8 == 0:
            each = cols // count
            cuts = [(0, rows, k * each, each) for k in range(count)]
        else:
            cuts = [(0, rows, 0, cols)]
        for cut in cuts:
            pieces.append((m, *cut, large % 2))
            small = rows * cols < 2048
            waves.append(0 if small else large // 4)
            large += 0 if small else 1
    return pieces, waves


class Place:
    def __init__(self, nd, nf):
        self.d = lax.axis_index("dp")
        self.f = lax.axis_index("fsdp")
        self.axes = [("f", b) for b in range(nf - 1, -1, -1)] + [
            ("d", b) for b in range(nd - 1, -1, -1)
        ]

    def bit(self, axis):
        value = self.f if axis[0] == "f" else self.d
        return lax.rem(value // (1 << axis[1]), 2)

    def partner(self, axis):
        step = (1 << axis[1]) * (1 - 2 * self.bit(axis))
        if axis[0] == "f":
            return (self.d, self.f + step)
        return (self.d + step, self.f)

    def index(self, whole, flip=None):
        picked = []
        for axis in self.axes:
            if axis in whole:
                picked.append(slice(None))
            elif axis == flip:
                picked.append(1 - self.bit(axis))
            else:
                picked.append(self.bit(axis))
        return tuple(picked)

    def barrier(self):
        sem = pltpu.get_barrier_semaphore()
        for axis in self.axes:
            pl.semaphore_signal(
                sem, inc=1, device_id=self.partner(axis), device_id_type=MESH_IDS
            )
        pl.semaphore_wait(sem, len(self.axes))


class Gather:
    def __init__(self, arrays):
        self.arrays = arrays
        self.given = arrays
        self.made = []
        self.nd, self.nf = mesh_bits()
        orders = hop_orders(self.nd, self.nf)
        self.cuts, self.waves = cut_pieces([a.shape for a in arrays])
        self.routes = [tuple(orders[cut[-1]]) + (CORE,) for cut in self.cuts]
        self.hops = self.nd + self.nf
        lead = (2,) * self.hops
        self.out_shape = [jax.ShapeDtypeStruct(lead + a.shape, a.dtype) for a in arrays]
        self.out_specs = [ANYWHERE] * len(arrays)
        count = len(self.cuts)
        self.scratch = [
            pltpu.SemaphoreType.DMA((count,)),
            pltpu.SemaphoreType.DMA((count, self.hops)),
            pltpu.SemaphoreType.DMA((count, self.hops)),
        ]

    def sizes(self, k):
        m, row, rows, col, cols, _ = self.cuts[k]
        block = rows * cols * self.arrays[m].dtype.itemsize
        return [block << h for h in range(self.hops)]

    def window(self, k):
        m, row, rows, col, cols, _ = self.cuts[k]
        return (pl.ds(row, rows), pl.ds(col, cols))

    def bind(self, place, ins, outs, scratch):
        self.place, self.ins, self.outs = place, ins, outs
        self.local_sem, self.send_sem, self.recv_sem = scratch

    def local(self, k):
        m = self.cuts[k][0]
        return pltpu.make_async_copy(
            self.ins[m].at[self.window(k)],
            self.outs[m].at[self.place.index(()) + self.window(k)],
            self.local_sem.at[k],
        )

    def hop(self, k, h):
        m, route = self.cuts[k][0], self.routes[k]
        region = self.outs[m].at[self.place.index(route[:h]) + self.window(k)]
        return pltpu.make_async_remote_copy(
            src_ref=region,
            dst_ref=region,
            send_sem=self.send_sem.at[k, h],
            recv_sem=self.recv_sem.at[k, h],
            device_id=self.place.partner(route[h]),
            device_id_type=MESH_IDS,
        )

    def start(self):
        for k in range(len(self.cuts)):
            self.local(k).start()

    def step(self, k, h):
        if h == 0:
            self.local(k).wait()
        else:
            self.hop(k, h - 1).wait_recv()
        if h < self.hops:
            self.hop(k, h).start()
        else:
            for g in range(self.hops):
                self.hop(k, g).wait_send()


def add_blocks(acc, index, window, incoming):
    lead = incoming.shape[:-2]
    outer, inner = lead[:-2], lead[-2:]

    def one(i, carry):
        first = []
        for size in reversed(outer):
            first.append(lax.rem(i, size))
            i = i // size
        first = first[::-1]
        for j in range(math.prod(inner)):
            at, rest = [], j
            for size in reversed(inner):
                at.append(rest % size)
                rest //= size
            at = tuple(first + at[::-1])
            left = list(at)
            where = tuple(left.pop(0) if isinstance(p, slice) else p for p in index) + window
            acc[where] = acc[where] + incoming[at]
        return carry

    lax.fori_loop(0, math.prod(outer), one, 0)


class Reduce:
    def __init__(self, given, made=None):
        made = made or {}
        self.given = given
        self.made = list(made)
        arrays = list(given) + list(made.values())
        self.arrays = arrays
        self.nd, self.nf = mesh_bits()
        orders = hop_orders(self.nd, self.nf)
        self.hops = self.nd + self.nf
        self.cuts, self.waves = cut_pieces([a.shape[-2:] for a in arrays])
        self.routes = [(CORE,) + tuple(reversed(orders[cut[-1]])) for cut in self.cuts]
        self.scratch = []
        for m, row, rows, col, cols, _ in self.cuts:
            for h in range(-1 if m < len(self.given) else 0, self.hops):
                free = self.hops - 1 - max(h, 0)
                self.scratch.append(pltpu.VMEM((2,) * free + (rows, cols), arrays[m].dtype))
        count = len(self.cuts)
        self.scratch += [
            pltpu.SemaphoreType.DMA((count,)),
            pltpu.SemaphoreType.DMA((count, self.hops)),
            pltpu.SemaphoreType.DMA((count, self.hops)),
        ]
        shapes = [a.shape[-2:] for a in arrays]
        self.out_shape = [jax.ShapeDtypeStruct(s, jnp.float32) for s in shapes]
        self.out_specs = [pl.BlockSpec(s, lambda *_: (0, 0)) for s in shapes]

    def sizes(self, k):
        m, row, rows, col, cols, _ = self.cuts[k]
        block = rows * cols * self.arrays[m].dtype.itemsize
        return [block << (self.hops - 1 - h) for h in range(self.hops)]

    def window(self, k):
        m, row, rows, col, cols, _ = self.cuts[k]
        return (pl.ds(row, rows), pl.ds(col, cols))

    def bind(self, place, ins, outs, scratch):
        self.place, self.ins, self.outs = place, ins, outs
        self.local_sem, self.send_sem, self.recv_sem = scratch[-3:]
        rest = list(scratch[:-3])
        self.accs, self.temps = [], []
        for m, *_ in self.cuts:
            self.accs.append(rest.pop(0) if m < len(self.given) else None)
            self.temps.append([rest.pop(0) for _ in range(self.hops)])
        self.rest = [axis for axis in place.axes if axis != CORE]

    def local(self, k):
        source = self.ins[self.cuts[k][0]].at[self.place.index(self.rest) + self.window(k)]
        return pltpu.make_async_copy(source, self.accs[k], self.local_sem.at[k])

    def within(self, k, h, flip=None):
        full = self.place.index(self.routes[k][h + 1 :], flip)
        if self.accs[k] is None:
            m, row, rows, col, cols, _ = self.cuts[k]
            return self.ins[m], full, (slice(row, row + rows), slice(col, col + cols))
        return self.accs[k], tuple(p for p, a in zip(full, self.place.axes) if a != CORE), ()

    def hop(self, k, h):
        m, route = self.cuts[k][0], self.routes[k]
        if h == 0:
            region = self.ins[m].at[self.place.index(route[1:], CORE) + self.window(k)]
        else:
            acc, index, window = self.within(k, h, route[h])
            region = acc.at[index + window]
        return pltpu.make_async_remote_copy(
            src_ref=region,
            dst_ref=self.temps[k][h],
            send_sem=self.send_sem.at[k, h],
            recv_sem=self.recv_sem.at[k, h],
            device_id=self.place.partner(route[h]),
            device_id_type=MESH_IDS,
        )

    def start(self):
        pass

    def step(self, k, h):
        own = self.accs[k] is not None
        if h == 0 and own:
            self.local(k).start()
        if h > 0:
            self.hop(k, h - 1).wait_recv()
            if h == 1 and own:
                self.local(k).wait()
            acc, index, window = self.within(k, h - 1)
            if h < self.hops:
                add_blocks(acc, index, window, self.temps[k][h - 1])
            else:
                m, row, rows, col, cols, _ = self.cuts[k]
                last = acc[index + window].astype(jnp.float32)
                last = last + self.temps[k][h - 1][...].astype(jnp.float32)
                self.outs[m][row : row + rows, col : col + cols] = last
        if h < self.hops:
            self.hop(k, h).start()
        else:
            for g in range(self.hops):
                self.hop(k, g).wait_send()


LINK_RATE = 46e3
CORE_RATE = 380e3
LATENCY = 2.5


class Phase:
    def __init__(self, run, steps, marks, needs=(), makes=()):
        self.run, self.steps, self.marks = run, steps, marks
        self.needs, self.makes = set(needs), set(makes)


def plan_steps(jobs, phases):
    order = []
    for j, job in enumerate(jobs):
        order += sorted(
            (wave + h, wave, (j, k), h)
            for k, wave in enumerate(job.waves)
            for h in range(job.hops + 1)
        )
    times, first, after = [], [], {}
    clock = 0.0
    for phase in phases:
        first.append(len(times))
        for _ in range(phase.steps):
            times += [clock + mark for mark in phase.marks]
            clock += phase.marks[-1]
        for m in phase.makes:
            after[len(jobs) - 1, m] = len(times)
    total = len(times)
    limit = [total] * len(order)
    for phase, begin in zip(phases, first):
        last = -1
        for i, (_, _, n, h) in enumerate(order):
            j, k = n
            if j == 0 and h == jobs[j].hops and jobs[j].cuts[k][0] in phase.needs:
                last = i
        for i in range(last + 1):
            limit[i] = min(limit[i], begin)
    waiting, active, done = {}, {}, {}
    now = 0.0

    def advance(key, until):
        nonlocal now
        while key not in done and now < until:
            for axis, queue in waiting.items():
                if queue and axis not in active:
                    active[axis] = queue.pop(0)
            far = any(axis[0] == "d" and axis[1] > 2 for axis in active)
            rates, span = {}, until - now
            for axis, (_, left) in active.items():
                halved = far and axis[0] == "d" and axis[1] > 1
                rates[axis] = CORE_RATE if axis == CORE else LINK_RATE / (2 if halved else 1)
                span = min(span, left / rates[axis])
            now += span
            for axis in list(active):
                active[axis][1] -= span * rates[axis]
                if active[axis][1] <= 1e-3:
                    done[active.pop(axis)[0]] = now + LATENCY

    slots = [[] for _ in range(total)]
    tail = []
    at, late = 0, 0.0
    for i, (_, _, n, h) in enumerate(order):
        j, k = n
        job = jobs[j]
        ready = now
        if h:
            advance((n, h - 1), math.inf)
            ready = max(ready, done[n, h - 1])
        else:
            at = max(at, after.get((j, job.cuts[k][0]), 0))
        while at < min(limit[i], total) and times[at] + late < ready - 0.3:
            at += 1
        if at < total:
            slots[at].append((n, h))
            late += max(ready - times[at] - late, 0.0)
            ready = max(ready, times[at] + late)
        else:
            tail.append((n, h))
        advance(None, ready)
        if h < job.hops:
            waiting.setdefault(job.routes[k][h], []).append([(n, h), float(job.sizes(k)[h])])
    return slots, tail


class Names:
    def __init__(self, names, refs):
        for name, ref in zip(names, refs):
            setattr(self, name, ref)


def carrying_kernel(phases, jobs, plan, names, *refs):
    spans, start = [], 0
    for count in [len(group) for group in names]:
        spans.append(refs[start : start + count])
        start += count
    given, landed, worked = [], [], []
    for kind, parts in ((given, 1), (landed, 3), (worked, 5)):
        rest = list(spans[parts])
        for job in jobs:
            count = (len(job.given), len(job.out_shape), len(job.scratch))[parts // 2]
            kind.append([rest.pop(0) for _ in range(count)])
    r = Names(names[0] + names[2] + names[4], spans[0] + spans[2] + spans[4])
    now = pl.program_id(0)
    slots, tail = plan
    place = Place(jobs[0].nd, jobs[0].nf)
    r.gathered = landed[0]
    for job, ins, outs, scratch in zip(jobs, given, landed, worked):
        job.bind(place, ins + [getattr(r, name) for name in job.made], outs, scratch)

    def run(items, opening=False):
        if opening:
            for job in jobs:
                job.start()
            place.barrier()
        for (j, k), h in items:
            jobs[j].step(k, h)

    base, begin = 0, 0
    for phase in phases:
        ticks = len(phase.marks)

        def one(phase=phase, base=base, begin=begin, ticks=ticks):
            passed = [0]

            def tick():
                t = passed[0]
                passed[0] += 1
                for s in range(phase.steps):
                    items = slots[base + s * ticks + t]
                    opening = base + s * ticks + t == 0
                    if items or opening:
                        pl.when(now == begin + s)(functools.partial(run, items, opening))

            phase.run(r, now - begin, tick)
            assert passed[0] == ticks

        pl.when((now >= begin) & (now < begin + phase.steps))(one)
        base += ticks * phase.steps
        begin += phase.steps
    if tail:
        pl.when(now == begin - 1)(functools.partial(run, tail))


def carry(phases, ins, outs, scratch, jobs, ident):
    plan = plan_steps(jobs, phases)
    given = [array for job in jobs for array in job.given]
    landed = [shape for job in jobs for shape in job.out_shape]
    worked = [item for job in jobs for item in job.scratch]
    names = (
        list(ins),
        [None] * len(given),
        list(outs),
        [None] * len(landed),
        list(scratch),
        [None] * len(worked),
    )
    results = pl.pallas_call(
        functools.partial(carrying_kernel, phases, jobs, plan, names),
        grid=(sum(phase.steps for phase in phases),),
        in_specs=[spec for _, spec in ins.values()] + [ANYWHERE] * len(given),
        out_specs=[spec for _, spec in outs.values()]
        + [spec for job in jobs for spec in job.out_specs],
        out_shape=[shape for shape, _ in outs.values()] + landed,
        scratch_shapes=list(scratch.values()) + worked,
        compiler_params=pltpu.CompilerParams(
            collective_id=ident, has_side_effects=True, vmem_limit_bytes=VMEM_LIMIT
        ),
    )(*[array for array, _ in ins.values()], *given)
    r = Names(list(outs), results)
    r.landed, rest = [], list(results[len(outs) :])
    for job in jobs:
        r.landed.append([rest.pop(0) for _ in job.out_shape])
    return r


def dot_nn(a, b):
    return lax.dot_general(a, b, (((1,), (0,)), ((), ())), preferred_element_type=jnp.float32)


def dot_nt(a, b):
    return lax.dot_general(a, b, (((1,), (1,)), ((), ())), preferred_element_type=jnp.float32)


def dot_tn(a, b):
    return lax.dot_general(a, b, (((0,), (0,)), ((), ())), preferred_element_type=jnp.float32)


def low(value):
    return value.astype(jnp.bfloat16)


def times(value, matrix):
    parts = [dot_nn(value, matrix[f]) for f in range(matrix.shape[0])]
    return parts[0] if len(parts) == 1 else jnp.concatenate(parts, axis=1)


def times_back(value, matrix):
    cols = matrix.shape[2]
    total = None
    for f in range(matrix.shape[0]):
        term = dot_nt(value[:, f * cols : (f + 1) * cols], matrix[f])
        total = term if total is None else total + term
    return total


def fixed(shape):
    return pl.BlockSpec(shape, lambda i: (0,) * len(shape))


def resident(array):
    zeros = (0,) * array.ndim
    return (array, pl.BlockSpec(array.shape, lambda i: zeros, pipeline_mode=pl.Buffered(1)))


def during(begin, steps, block, axis=0):
    def index(i):
        at = jnp.minimum(jnp.maximum(i - begin, 0), steps - 1)
        return tuple(at if d == axis else 0 for d in range(len(block)))

    return pl.BlockSpec(block, index)


def struct(shape, dtype):
    return jax.ShapeDtypeStruct(shape, dtype)


def rows_at(step, size):
    return pl.ds(pl.multiple_of(step * size, size), size)


def fetch(pairs, sems):
    copies = [
        pltpu.make_async_copy(source, target, sems.at[n])
        for n, (source, target) in enumerate(pairs)
    ]
    for copy in copies:
        copy.start()
    for copy in copies:
        copy.wait()


ROW_PAIRS = 2


def softmax(scores, axis):
    top = jnp.max(scores, axis=axis, keepdims=True)
    weight = jnp.exp(scores - top)
    return weight * (1.0 / jnp.sum(weight, axis=axis, keepdims=True))


def gelu_pair(x):
    below = 0.5 + 0.5 * lax.erf(x * (1.0 / math.sqrt(2.0)))
    bell = jnp.exp(-0.5 * x * x) * (1.0 / math.sqrt(2.0 * math.pi))
    return x * below, below + x * bell


def row_mean(value):
    return jnp.mean(value, axis=-1, keepdims=True)


def col_sum(value):
    return jnp.sum(value, axis=0, keepdims=True)


def own_image(r, p):
    return r.owner[p]


def flat(ref):
    return ref.reshape(-1, ref.shape[-1])


def merged(ref, blocks, rows):
    return ref.reshape(blocks, rows, ref.shape[-1])


def put_half(out, half, x, d):
    cols = out.shape[-1]
    nf = bits_of(lax.axis_size("fsdp"))
    whole = low(dot_tn(x, d))
    for f in range(1 << nf):
        at = tuple((f >> b) % 2 for b in range(nf - 1, -1, -1))
        part = whole[:, f * cols : (f + 1) * cols]
        out[at + (half,)] = part.reshape(out.shape[nf + 1 :])


def project_keys_phase(r, step, tick):
    tick()

    @pl.when(step == 0)
    def _():
        targets = (r.w_tk, r.w_tv, r.w_iq)
        fetch([(g.reshape(w.shape), w) for g, w in zip(r.gathered, targets)], r.sems)
        images, real = r.states.shape[:2]
        r.image[...] = jnp.zeros_like(r.image)
        for i in range(images):
            r.image[i, :real, :] = r.states[i]
            r.region_counts[i] = lax.fori_loop(
                0, real, lambda k, total, i=i: total + r.mask[i, k], 0
            )
        r.image_rows[...] = r.image[...]
        r.iq[...] = low(times(flat(r.image[...]), r.w_iq)).reshape(r.iq.shape)

    here = rows_at(step, r.text.shape[0] // r.owner.shape[0] * ROW_PAIRS)
    rows = r.text[here, :]
    r.tk[here, :] = low(times(rows, r.w_tk))
    r.tv[here, :] = low(times(rows, r.w_tv))
    tick()


def attend_image_phase(r, step, tick):
    tick()
    regions, length = r.iprob.shape[1:]
    heads = r.tk.shape[1] // HDIM
    columns = [slice(h * HDIM, (h + 1) * HDIM) for h in range(heads)]
    scale = 1.0 / math.sqrt(HDIM)
    for q in range(ROW_PAIRS):
        p = step * ROW_PAIRS + q
        mine = own_image(r, p)
        here, rows_i = rows_at(p, length), rows_at(p, regions)
        kept = lax.broadcasted_iota(jnp.int32, (regions, length), 1) < r.lens[p]
        scores = [scale * dot_nt(r.iq[mine, :, at], r.tk[here, at]) for at in columns]
        probs = [softmax(jnp.where(kept, one, masked_score), 1) for one in scores]
        for h in range(heads):
            r.iprob[p * heads + h] = probs[h]
        parts = [low(dot_nn(low(one), r.tv[here, at])) for one, at in zip(probs, columns)]
        r.ictx[rows_i, :] = jnp.concatenate(parts, axis=1)
        tick()


def attend_text_phase(r, step, tick):
    tick()

    @pl.when(step == 0)
    def _():
        targets = (r.w_tq, r.w_ik, r.w_iv)
        fetch([(g.reshape(w.shape), w) for g, w in zip(r.gathered[7:], targets)], r.sems)
        rows = flat(r.image[...])
        for w, out in ((r.w_ik, r.ik), (r.w_iv, r.iv)):
            out[...] = low(times(rows, w)).reshape(out.shape)

    regions, length = r.tprob.shape[1:]
    heads = r.tq.shape[1] // HDIM
    columns = [slice(h * HDIM, (h + 1) * HDIM) for h in range(heads)]
    scale = 1.0 / math.sqrt(HDIM)
    r.tq[...] = low(times(r.text[rows_at(step, r.tq.shape[0]), :], r.w_tq))
    tick()
    for q in range(ROW_PAIRS):
        mine = own_image(r, step * ROW_PAIRS + q)
        here = slice(q * length, (q + 1) * length)
        row = lax.broadcasted_iota(jnp.int32, (regions, length), 0)
        kept = row < r.region_counts[mine]
        scores = [scale * dot_nt(r.ik[mine, :, at], r.tq[here, at]) for at in columns]
        probs = [softmax(jnp.where(kept, one, masked_score), 0) for one in scores]
        for h in range(heads):
            r.tprob[q * heads + h] = probs[h]
        parts = [low(dot_tn(low(one), r.iv[mine, :, at])) for one, at in zip(probs, columns)]
        r.tctx[here, :] = jnp.concatenate(parts, axis=1)
        tick()


def stream_rows(r, step, tick, limits, x, ctx, cot, norms, weights, keeps, outs):
    w_out, w_inner, w_outer = weights
    mid_ref, act_ref, hid_ref, ffn_ref, branch_ref = keeps
    out, dz_out, dctx_out, ngrad = outs
    rows = x.shape[0]
    group, real = cot.shape[:2]
    slots = rows // group

    def normalize(z):
        offset = z - row_mean(z)
        inv = lax.rsqrt(row_mean(offset * offset) + norm_eps)
        return offset * inv, inv

    def normalize_back(dy, xhat, inv, gain):
        dx = dy * gain
        return inv * (dx - row_mean(dx) - xhat * row_mean(dx * xhat))

    @pl.when(step == 0)
    def _():
        ngrad[...] = jnp.zeros_like(ngrad)
        if real < slots:
            r.cot_wide[...] = jnp.zeros_like(r.cot_wide)

    row = lax.broadcasted_iota(jnp.int32, (rows, 1), 0)
    kept = row < 0
    for q in range(group):
        inside = (row >= q * slots) & (row < q * slots + limits(step * group + q))
        kept = kept | inside
        if real < slots:
            r.cot_wide[q * slots : q * slots + real, :] = cot[q].astype(jnp.float32)
    kept = kept.astype(jnp.float32)
    first_hat, first_inv = normalize(x[...].astype(jnp.float32) + times(ctx[...], w_out))
    mid = first_hat * norms[0] + norms[1]
    mid_low = low(mid)
    mid_ref[...] = mid_low
    tick()
    cols = w_inner.shape[2]
    for f in range(w_inner.shape[0]):
        at = slice(f * cols, (f + 1) * cols)
        act, grad = gelu_pair(dot_nn(mid_low, w_inner[f]))
        act_ref[:, at] = low(act)
        hid_ref[:, at] = low(grad)
        tick()
    second_hat, second_inv = normalize(mid + times(act_ref[...], w_outer))
    result = low((second_hat * norms[2] + norms[3]) * kept)
    for q in range(group):
        out[q] = result[q * slots : q * slots + real]
    if real < slots:
        dy = r.cot_wide[...] * kept
    else:
        dy = cot[...].reshape(rows, -1).astype(jnp.float32) * kept
    second_dz = normalize_back(dy, second_hat, second_inv, norms[2])
    ffn_low = low(second_dz)
    ffn_ref[...] = ffn_low
    sums = [col_sum(dy * second_hat), col_sum(dy)]
    tick()
    hid_ref[...] = low(times_back(ffn_low, w_outer) * hid_ref[...].astype(jnp.float32))
    tick()
    mid_grad = second_dz + times_back(hid_ref[...], w_inner)
    first_dz = normalize_back(mid_grad, first_hat, first_inv, norms[0])
    dz_out[...] = first_dz
    branch_low = low(first_dz)
    branch_ref[...] = branch_low
    tick()
    dctx_out[...] = low(times_back(branch_low, w_out))
    sums = [col_sum(mid_grad * first_hat), col_sum(mid_grad)] + sums
    for n in range(4):
        ngrad[n : n + 1, :] += sums[n]
    tick()


def store_grad(out, x, d):
    cols = out.shape[2]
    whole = low(dot_tn(x, d))
    for f in range(out.shape[0]):
        out[f] = whole[:, f * cols : (f + 1) * cols]


def add_to(ref, mine, value):
    value = low(value).astype(jnp.float32)
    for i in range(ref.shape[0]):
        ref[i] += jnp.where(mine == i, value, 0.0)


def image_phase(first_col, norm_wide, r, step, tick):
    tick()
    group, slots, wide = r.cot.shape[0], r.image.shape[1], r.image.shape[2]

    @pl.when(step == 0)
    def _():
        targets = (r.w_io, r.w_ii, r.w_iu)
        fetch(
            [(g.reshape(w.shape), w) for g, w in zip(r.gathered[4:], targets)]
            + [(r.gathered[3], r.norm_parts)],
            r.sems,
        )
        parts = r.norm_parts.shape[0:-2]
        nf = bits_of(lax.axis_size("fsdp"))
        for i in range(math.prod(parts)):
            at, rest = [], i
            for _ in parts:
                at.append(rest % 2)
                rest //= 2
            at = at[::-1]
            f = sum(bit << k for k, bit in enumerate(reversed(at[:nf])))
            d = sum(bit << k for k, bit in enumerate(reversed(at[nf:])))
            first = (d * (1 << nf) + f) * norm_wide
            r.norms[:, first : first + norm_wide] = r.norm_parts[tuple(at)]

    for q in range(group):
        r.visual[q * slots : (q + 1) * slots, :] = r.image[own_image(r, step * group + q)]
    here = rows_at(step, group * slots)
    norms = [r.norms[n : n + 1, first_col : first_col + wide] for n in range(4)]
    stream_rows(
        r,
        step,
        tick,
        lambda p: r.region_counts[own_image(r, p)],
        r.visual,
        r.ictx.at[here],
        r.cot,
        norms,
        (r.w_io, r.w_ii, r.w_iu),
        [ref.at[here] for ref in (r.mid, r.act, r.hid, r.ffn, r.branch)],
        (r.image_out, r.image_dz, r.dctx.at[here], r.image_ngrad),
    )


def image_grads_phase(r, step, tick):
    tick()
    here = rows_at(step, r.g_io.shape[1])
    store_grad(r.g_io, r.ictx[:, here], r.branch[...])
    store_grad(r.g_ii, r.mid[:, here], r.hid[...])
    store_grad(r.g_iu, r.act[:, here], r.ffn[...])
    tick()


def back_image_phase(r, step, tick):
    tick()
    regions, length = r.iprob.shape[1:]
    heads = r.tk.shape[1] // HDIM
    columns = [slice(h * HDIM, (h + 1) * HDIM) for h in range(heads)]
    scale = 1.0 / math.sqrt(HDIM)

    @pl.when(step == 0)
    def _():
        r.diq_sum[...] = jnp.zeros_like(r.diq_sum)

    for q in range(ROW_PAIRS):
        p = step * ROW_PAIRS + q
        mine = own_image(r, p)
        here, rows_i = rows_at(p, length), rows_at(p, regions)
        local = slice(q * length, (q + 1) * length)
        dprobs = [dot_nt(r.dctx[rows_i, at], r.tv[here, at]) for at in columns]
        dvalues = [
            low(dot_tn(low(r.iprob[p * heads + h]), r.dctx[rows_i, at]))
            for h, at in enumerate(columns)
        ]
        dscores = []
        for h in range(heads):
            probs = r.iprob[p * heads + h]
            inner = jnp.sum(probs * dprobs[h], axis=1, keepdims=True)
            dscores.append(low(probs * (dprobs[h] - inner)))
        parts = [scale * dot_nn(one, r.tk[here, at]) for one, at in zip(dscores, columns)]
        add_to(r.diq_sum, mine, jnp.concatenate(parts, axis=1))
        dkeys = [
            low(scale * dot_tn(one, r.iq[mine, :, at])) for one, at in zip(dscores, columns)
        ]
        for ref, out, values in ((r.tv, r.dtv, dvalues), (r.tk, r.dtk, dkeys)):
            values = jnp.concatenate(values, axis=1)
            ref[here, :] = values
            out[local, :] = values
        tick()


def key_grads_phase(r, step, tick):
    tick()
    diq = low(r.diq_sum[...])
    r.diq[...] = diq
    here = rows_at(step, r.g_iq.shape[1])
    store_grad(r.g_iq, flat(r.image[:, :, here]), flat(diq))
    here = rows_at(step, r.g_tk.shape[1])
    store_grad(r.g_tk, r.text[:, here], r.tk[...])
    store_grad(r.g_tv, r.text[:, here], r.tv[...])
    tick()


def text_phase(r, step, tick):
    tick()
    rows = r.x.shape[0]
    here = rows_at(step, rows)
    norms = [r.norms[n : n + 1, : r.x.shape[1]] for n in range(4)]
    stream_rows(
        r,
        step,
        tick,
        lambda p: r.lens[p],
        r.x,
        r.tctx.at[here],
        r.cot,
        norms,
        (r.w_to, r.w_ti, r.w_tu),
        [ref.at[here] for ref in (r.mid, r.act, r.hid, r.ffn, r.branch)],
        (r.text_out, r.text_dz, r.dctx, r.text_ngrad),
    )


def grad_phase(out, x, d, r, step, tick):
    tick()
    out = getattr(r, out)
    here = rows_at(step, out.shape[1])
    store_grad(out, getattr(r, x)[:, here], getattr(r, d)[...])
    tick()


def back_text_phase(r, step, tick):
    tick()
    regions, length = r.tprob.shape[1:]
    heads = r.tq.shape[1] // HDIM
    columns = [slice(h * HDIM, (h + 1) * HDIM) for h in range(heads)]
    scale = 1.0 / math.sqrt(HDIM)

    @pl.when(step == 0)
    def _():
        r.dik_sum[...] = jnp.zeros_like(r.dik_sum)
        r.div_sum[...] = jnp.zeros_like(r.div_sum)

    for q in range(ROW_PAIRS):
        p = step * ROW_PAIRS + q
        mine = own_image(r, p)
        here = rows_at(p, length)
        local = slice(q * length, (q + 1) * length)
        dprobs = [dot_nt(r.iv[mine, :, at], r.dtc[local, at]) for at in columns]
        parts = [
            dot_nn(low(r.tprob[q * heads + h]), r.dtc[local, at]) for h, at in enumerate(columns)
        ]
        add_to(r.div_sum, mine, jnp.concatenate(parts, axis=1))
        dscores = []
        for h in range(heads):
            probs = r.tprob[q * heads + h]
            inner = jnp.sum(probs * dprobs[h], axis=0, keepdims=True)
            dscores.append(low(probs * (dprobs[h] - inner)))
        parts = [scale * dot_nn(one, r.tq[local, at]) for one, at in zip(dscores, columns)]
        add_to(r.dik_sum, mine, jnp.concatenate(parts, axis=1))
        parts = [
            low(scale * dot_tn(one, r.ik[mine, :, at])) for one, at in zip(dscores, columns)
        ]
        r.dtq[here, :] = jnp.concatenate(parts, axis=1)
        tick()


def query_grads_phase(r, step, tick):
    tick()
    here = rows_at(step, r.text.shape[1] // 2)
    put_half(r.g_tq, step, r.text[:, here], r.dtq[...])
    dik, div = low(r.dik_sum[...]), low(r.div_sum[...])
    r.dik[...] = dik
    r.div[...] = div
    here = rows_at(step, r.image.shape[2] // 2)
    columns = flat(r.image[:, :, here])
    put_half(r.g_ik, step, columns, flat(dik))
    put_half(r.g_iv, step, columns, flat(div))
    tick()


def data_grads_phase(r, step, tick):
    images, real = r.image_grad.shape[:2]
    pairs = r.owner.shape[0]
    slots = r.image_dz.shape[0] // pairs
    tick()

    @pl.when(step == 0)
    def _():
        for i in range(images):
            total = jnp.zeros((slots, r.image_dz.shape[1]), jnp.float32)
            for p in range(pairs):
                rows = r.image_dz[p * slots : (p + 1) * slots, :]
                total += jnp.where(own_image(r, p) == i, rows, 0.0)
            for d, w in ((r.diq, r.w_iq), (r.dik, r.w_ik), (r.div, r.w_iv)):
                total = total + times_back(d[i], w)
            r.image_grad[i] = total[:real]

    total = r.text_dz[...]
    here = rows_at(step, total.shape[0])
    for d, w in ((r.dtq.at[here], r.w_tq), (r.dtk, r.w_tk), (r.dtv, r.w_tv)):
        total = total + times_back(d[...], w)
        tick()
    r.text_grad[...] = total


def pass_kernel(count, *refs):
    for source, target in zip(refs[:count], refs[count:]):
        target[...] = source[...]


def pass_on(arrays):
    return pl.pallas_call(
        functools.partial(pass_kernel, len(arrays)),
        out_shape=[struct(a.shape, a.dtype) for a in arrays],
        in_specs=[WHOLE] * len(arrays),
        out_specs=[WHOLE] * len(arrays),
        compiler_params=pltpu.CompilerParams(vmem_limit_bytes=VMEM_LIMIT),
    )(*arrays)


def whole_weight(shard, block):
    nd, nf = mesh_bits()
    rows, cols = shard.shape
    block = block.reshape(1 << nf, rows << nd, cols)
    if cols % 128:
        block = jnp.swapaxes(block, 0, 1).reshape(1, rows << nd, cols << nf)
    return block


def device_blocks(grad, shard):
    nd, nf = mesh_bits()
    rows, cols = shard.shape
    if cols % 128:
        grad = jnp.swapaxes(grad.reshape(rows << nd, 1 << nf, cols), 0, 1)
    return grad.reshape((2,) * (nd + nf) + (rows, cols))


def norm_blocks(rows):
    nd, nf = mesh_bits()
    wide = rows.shape[1] >> (nd + nf)
    split = rows.reshape(4, 1 << nd, 1 << nf, wide).transpose(2, 1, 0, 3)
    split = jnp.pad(split, ((0, 0), (0, 0), (0, 4), (0, 128 - wide)))
    return split.reshape((2,) * (nd + nf) + (8, 128))


def body(
    text_states,
    image_states,
    text_lengths,
    region_mask,
    group_ids,
    image_query,
    image_key,
    image_value,
    text_query,
    text_key,
    text_value,
    image_output,
    text_output,
    image_inner,
    image_outer,
    text_inner,
    text_outer,
    norm_params,
    cot_text,
    cot_image,
):
    nd, nf = mesh_bits()
    lead = (2,) * (nd + nf)
    bf, f32 = jnp.bfloat16, jnp.float32
    pairs, length, width_text = text_states.shape
    images, regions, width_image = image_states.shape
    padded = -(-regions // 16) * 16
    wide = image_query.shape[1] << nf
    heads = wide // HDIM
    rows_text, rows_image = pairs * length, pairs * padded
    norm_wide = norm_params.shape[1]
    device = lax.axis_index("dp") * lax.axis_size("fsdp") + lax.axis_index("fsdp")
    owner = group_ids - device * images
    text = text_states.reshape(rows_text, width_text)
    def full(shard):
        rows, cols = shard.shape
        return pltpu.VMEM((1 << nf, rows << nd, cols), bf)

    def vmem(rows, cols, dtype=bf):
        return pltpu.VMEM((rows, cols), dtype)

    n = ROW_PAIRS
    steps = pairs // n
    group = pairs // 2
    block_i = group * padded
    gather = Gather(
        [text_key, text_value, image_query, norm_params, image_output, image_inner, image_outer]
        + [text_query, image_key, image_value, text_output, text_inner, text_outer]
    )
    phases, begin = [], [0]

    def phase(run, count, marks, **kw):
        phases.append(Phase(run, count, marks, **kw))
        begin.append(begin[-1] + count)
        return begin[-2]

    phase(project_keys_phase, steps, (0.0, 1.4), needs=range(3))
    phase(attend_image_phase, steps, (0.0, 1.9, 3.8))
    stages = 1 << nf
    marks = [0.0, 1.1] + [1.1 + 1.0 * (k + 1) / stages for k in range(stages)]
    marks += [3.3, 4.4, 5.7, 6.4]
    at_image = phase(
        functools.partial(image_phase, width_text, norm_wide), 2, marks, needs=range(3, 7)
    )
    at_image_grads = phase(image_grads_phase, 4, (0.0, 1.0))
    at_back = phase(back_image_phase, steps, (0.0, 2.3, 4.6))
    at_grads = phase(key_grads_phase, 2, (0.0, 4.2))
    at_attend = phase(attend_text_phase, steps, (0.0, 0.8, 2.8, 4.8), needs=range(7, 10))
    third = width_text // 3

    def grad_out(weight_shard, inner, first, count, size):
        shape = (1 << nf, inner, weight_shard.shape[1])
        if weight_shard.shape[1] % 128:
            shape = (1, inner, weight_shard.shape[1] << nf)
        block = (shape[0], size, shape[2])
        return (struct(shape, bf), during(first, count, block, 1))

    by_pair = during(at_image, 2, (group, regions, width_image))
    probs = during(at_attend, steps, (n * heads, padded, length))
    pair_rows = during(at_attend, steps, (n * length, wide))
    back_rows = during(at_back, steps, (n * length, wide))
    image_shape = (images, padded, wide)
    a = carry(
        phases,
        dict(
            lens=(text_lengths, SCALARS),
            owner=(owner, SCALARS),
            mask=(region_mask, SCALARS),
            text=resident(text),
            states=resident(image_states),
            cot=(cot_image, by_pair),
        ),
        dict(
            ik=(struct(image_shape, bf), fixed(image_shape)),
            iv=(struct(image_shape, bf), fixed(image_shape)),
            tq=(struct((rows_text, wide), bf), pair_rows),
            tprob=(struct((pairs * heads, padded, length), f32), probs),
            tctx=(struct((rows_text, wide), bf), pair_rows),
            image_rows=(
                struct((images, padded, width_image), bf),
                fixed((images, padded, width_image)),
            ),
            norms=(struct((4, norm_wide << (nd + nf)), f32), fixed((4, norm_wide << (nd + nf)))),
            image_out=(struct(cot_image.shape, bf), by_pair),
            image_dz=(
                struct((rows_image, width_image), f32),
                during(at_image, 2, (block_i, width_image)),
            ),
            image_ngrad=(struct((4, width_image), f32), fixed((4, width_image))),
            dtk=(struct((rows_text, wide), bf), back_rows),
            dtv=(struct((rows_text, wide), bf), back_rows),
            diq=(struct(image_shape, bf), fixed(image_shape)),
            g_io=grad_out(image_output, wide, at_image_grads, 4, wide // 4),
            g_ii=grad_out(image_inner, width_image, at_image_grads, 4, width_image // 4),
            g_iu=grad_out(image_outer, width_image, at_image_grads, 4, width_image // 4),
            g_iq=grad_out(image_query, width_image, at_grads, 2, width_image // 2),
            g_tk=grad_out(text_key, width_text, at_grads, 2, width_text // 2),
            g_tv=grad_out(text_value, width_text, at_grads, 2, width_text // 2),
        ),
        dict(
            w_tq=full(text_query),
            w_tk=full(text_key),
            w_tv=full(text_value),
            w_iq=full(image_query),
            w_ik=full(image_key),
            w_iv=full(image_value),
            w_io=full(image_output),
            w_ii=full(image_inner),
            w_iu=full(image_outer),
            image=pltpu.VMEM((images, padded, width_image), bf),
            visual=vmem(block_i, width_image),
            region_counts=pltpu.SMEM((images,), jnp.int32),
            norm_parts=pltpu.VMEM(lead + norm_params.shape, f32),
            sems=pltpu.SemaphoreType.DMA((4,)),
            iq=pltpu.VMEM(image_shape, bf),
            tk=vmem(rows_text, wide),
            tv=vmem(rows_text, wide),
            iprob=pltpu.VMEM((pairs * heads, padded, length), f32),
            ictx=vmem(rows_image, wide),
            mid=vmem(rows_image, width_image),
            act=vmem(rows_image, width_image),
            hid=vmem(rows_image, width_image),
            ffn=vmem(rows_image, width_image),
            branch=vmem(rows_image, width_image),
            dctx=vmem(rows_image, wide),
            diq_sum=pltpu.VMEM(image_shape, f32),
            cot_wide=vmem(block_i, width_image, f32),
        ),
        [gather],
        0,
    )
    whole = [whole_weight(s, g) for s, g in zip(gather.given, a.landed[0]) if s is not norm_params]
    w_tk, w_tv, w_iq, _, _, _, w_tq, w_ik, w_iv, w_to, w_ti, w_tu = whole

    job = Reduce(
        [
            device_blocks(grad, shard)
            for grad, shard in (
                (a.g_io, image_output),
                (a.g_ii, image_inner),
                (a.g_iu, image_outer),
                (a.g_iq, image_query),
                (a.g_tk, text_key),
                (a.g_tv, text_value),
            )
        ]
    )
    phases, begin = [], [0]
    inner = w_ti.shape[0] * w_ti.shape[2]
    block_t = n * length
    stages = w_ti.shape[0]
    marks = [0.0, 1.6] + [1.6 + 3.6 * (k + 1) / stages for k in range(stages)]
    marks += [7.8, 9.8, 11.8, 12.6]
    at_text = phase(text_phase, steps, marks)
    at_tu = phase(functools.partial(grad_phase, "g_tu", "act", "ffn"), 12, (0.0, 0.7))
    at_ti = phase(functools.partial(grad_phase, "g_ti", "mid", "hid"), 6, (0.0, 1.4))
    at_to = phase(functools.partial(grad_phase, "g_to", "tctx", "branch"), 4, (0.0, 0.8))
    by_pair = during(at_text, steps, (n, length, width_text))

    def text_rows(cols):
        return during(at_text, steps, (block_t, cols))

    b = carry(
        phases,
        dict(
            lens=(text_lengths, SCALARS),
            x=(text, text_rows(width_text)),
            tctx=resident(a.tctx),
            cot=(cot_text, by_pair),
            norms=resident(a.norms),
            w_to=resident(w_to),
            w_ti=resident(w_ti),
            w_tu=resident(w_tu),
        ),
        dict(
            text_out=(struct(cot_text.shape, bf), by_pair),
            text_dz=(struct((rows_text, width_text), f32), text_rows(width_text)),
            dctx=(struct((rows_text, wide), bf), text_rows(wide)),
            text_ngrad=(struct((4, width_text), f32), fixed((4, width_text))),
            g_tu=grad_out(text_outer, inner, at_tu, 12, inner // 12),
            g_ti=grad_out(text_inner, width_text, at_ti, 6, width_text // 6),
            g_to=grad_out(text_output, wide, at_to, 4, wide // 4),
        ),
        dict(
            mid=vmem(rows_text, width_text),
            act=vmem(rows_text, inner),
            hid=vmem(rows_text, inner),
            ffn=vmem(rows_text, width_text),
            branch=vmem(rows_text, width_text),
        ),
        [job],
        1,
    )
    o_io, o_ii, o_iu, o_iq, o_tk, o_tv = b.landed[0]

    norm_rows = norm_blocks(jnp.concatenate([b.text_ngrad, a.image_ngrad], axis=1))
    job = Reduce(
        [
            device_blocks(b.g_tu, text_outer),
            device_blocks(b.g_ti, text_inner),
            device_blocks(b.g_to, text_output),
            norm_rows,
        ],
        dict(
            g_tq=struct(lead + text_query.shape, bf),
            g_ik=struct(lead + image_key.shape, bf),
            g_iv=struct(lead + image_value.shape, bf),
        ),
    )
    phases, begin = [], [0]
    at_back = phase(back_text_phase, steps, (0.0, 2.3, 4.6))
    phase(query_grads_phase, 2, (0.0, 3.2), makes=range(4, 7))
    at_data = phase(data_grads_phase, steps, (0.0, 0.9, 1.8, 2.6))
    probs = during(at_back, steps, (n * heads, padded, length))
    back_rows = during(at_back, steps, (n * length, wide))
    data_rows = during(at_data, steps, (block_t, wide))
    data_out = during(at_data, steps, (block_t, width_text))
    c = carry(
        phases,
        dict(
            owner=(owner, SCALARS),
            ik=resident(a.ik),
            iv=resident(a.iv),
            tq=(a.tq, back_rows),
            tprob=(a.tprob, probs),
            dtc=(b.dctx, back_rows),
            text=resident(text),
            image=resident(a.image_rows),
            text_dz=(b.text_dz, data_out),
            dtk=(a.dtk, data_rows),
            dtv=(a.dtv, data_rows),
            image_dz=resident(a.image_dz),
            diq=resident(a.diq),
            w_tq=resident(w_tq),
            w_tk=resident(w_tk),
            w_tv=resident(w_tv),
            w_iq=resident(w_iq),
            w_ik=resident(w_ik),
            w_iv=resident(w_iv),
        ),
        dict(
            text_grad=(struct((rows_text, width_text), f32), data_out),
            image_grad=(struct(image_states.shape, f32), fixed(image_states.shape)),
        ),
        dict(
            dtq=vmem(rows_text, wide),
            dik=pltpu.VMEM(image_shape, bf),
            div=pltpu.VMEM(image_shape, bf),
            dik_sum=pltpu.VMEM(image_shape, f32),
            div_sum=pltpu.VMEM(image_shape, f32),
            g_tq=pltpu.VMEM(lead + text_query.shape, bf),
            g_ik=pltpu.VMEM(lead + image_key.shape, bf),
            g_iv=pltpu.VMEM(lead + image_value.shape, bf),
        ),
        [job],
        2,
    )
    o_tu, o_ti, o_to, o_norm, o_tq, o_ik, o_iv = c.landed[0]
    owned = pass_on([o_iq, o_ik, o_iv, o_tq, o_tk, o_tv, o_io, o_to, o_ii, o_iu, o_ti, o_tu])
    return (
        b.text_out,
        a.image_out,
        c.text_grad.reshape(text_states.shape),
        c.image_grad,
        *owned,
        o_norm[:4, :norm_wide],
    )


def solution(mesh):
    placed = (
        P(("dp", "fsdp"), None, None),
        P(("dp", "fsdp"), None, None),
        P(("dp", "fsdp")),
        P(("dp", "fsdp"), None),
        P(("dp", "fsdp")),
        P("dp", "fsdp"),
        P("dp", "fsdp"),
        P("dp", "fsdp"),
        P("dp", "fsdp"),
        P("dp", "fsdp"),
        P("dp", "fsdp"),
        P("dp", "fsdp"),
        P("dp", "fsdp"),
        P("dp", "fsdp"),
        P("dp", "fsdp"),
        P("dp", "fsdp"),
        P("dp", "fsdp"),
        P(None, ("dp", "fsdp")),
        P(("dp", "fsdp"), None, None),
        P(("dp", "fsdp"), None, None),
    )
    return jax.shard_map(
        body,
        mesh=mesh,
        in_specs=placed,
        out_specs=(
            P(("dp", "fsdp"), None, None),
            P(("dp", "fsdp"), None, None),
            P(("dp", "fsdp"), None, None),
            P(("dp", "fsdp"), None, None),
            P("dp", "fsdp"),
            P("dp", "fsdp"),
            P("dp", "fsdp"),
            P("dp", "fsdp"),
            P("dp", "fsdp"),
            P("dp", "fsdp"),
            P("dp", "fsdp"),
            P("dp", "fsdp"),
            P("dp", "fsdp"),
            P("dp", "fsdp"),
            P("dp", "fsdp"),
            P("dp", "fsdp"),
            P(None, ("dp", "fsdp")),
        ),
        check_vma=False,
    )
```

profile of v0, /device:TPU:0, one launch (start us, length us, event | category | flops | bytes accessed | tf_op | source)
XLA Modules:
  0.0 330.3 jit_solution(2147046670287432658)
XLA Ops:
  0.7 1.2 broadcast_subtract_fusion.refs_1_.refs_0_
  1.8 1.6 copy.37.refs_4_
  3.4 2.2 copy.38.refs_5_
  5.7 138.3 %shard_map.323 = (bf16[2,48,1024]{2,1,0:T(8,128)(2,1)}, bf16[2,48,1024]{2,1,0:T(8,128)(2,1)}, bf16[1024,1024]{1,0:T(8,128)(2,1)}, f32[64,48,128]{2,1,0:T(8,128)}...) custom-call(s32[8]{0:T(128)} %refs_0_.3, ...), custom_call_target="tpu_custom_call" | custom-call | tf_op jit(solution)/shard_map/pallas_call | solution.py:449
  143.9 0.0 copy-start.2
  143.9 82.1 %shard_map.324 = (bf16[8,128,768]{2,1,0:T(8,128)(2,1)}, f32[1024,768]{1,0:T(8,128)}, bf16[1024,1024]{1,0:T(8,128)(2,1)}, f32[4,768]{1,0:T(4,128)}, bf16[2,3072,3...) custom-call(s32[8]{0:T(128)} %refs_0_.3, ...), custom_call_target="tpu_custom_call" | custom-call | tf_op jit(solution)/shard_map/pallas_call | solution.py:449
  226.1 0.0 copy-done.2
  226.1 0.7 pad_maximum_fusion
  226.8 0.2 reshape.119
  227.0 0.7 pad.4
  227.7 0.0 copy-start.1
  227.7 91.1 %shard_map.325 = (f32[1024,768]{1,0:T(8,128)}, f32[2,36,1024]{2,1,0:T(8,128)}, f32[192,384]{1,0:T(8,128)}, f32[48,1536]{1,0:T(8,128)}, f32[64,384]{1,0:T(8,128)}...) custom-call(s32[8]{0:T(128)} %broadcast_subtract_fusion.refs_1_.refs_0_, ...), custom_call_target="tpu_custom_call" | custom-call | tf_op jit(solution)/shard_map/pallas_call | solution.py:449
  318.8 1.3 slice.3
  320.0 1.9 copy.41
  322.0 0.0 copy-done.1
  322.0 1.1 copy.40
  323.1 2.7 shard_map.326
  325.8 0.0 copy-start
  325.8 2.8 copy.46
  328.6 0.0 copy-done
  328.6 1.7 copy.47
  (1 shorter events, 0.0 us)
Async XLA Ops:
  143.9 82.1 %copy-start.2 = (f32[4,1024]{1,0:T(4,128)S(1)}, f32[4,1024]{1,0:T(4,128)}, u32[]{:S(2)}) copy-start(f32[4,1024]{1,0:T(4,128)} %get-tuple-element.113) | copy-start | bytes 49156
  227.7 94.3 %copy-start.1 = (bf16[8,36,1024]{2,1,0:T(8,128)(2,1)S(1)}, bf16[8,36,1024]{2,1,0:T(8,128)(2,1)}, u32[]{:S(2)}) copy-start(bf16[8,36,1024]{2,1,0:T(8,128)(2,1)} %get-tuple-element.142) | copy-start | bytes 1769476
  325.8 2.8 copy-start
where the time goes:
time: 331 us; the launch traced here: 330 us
  Pallas kernels  314 us (95%)
  local copies, waits for them, and re-layouts  13.5 us (4%)
    pallas_call x3, Pallas kernels, carry(): pl.pallas_call(functools.partial(carrying_kernel, phases, jobs, plan, nam...  311 us
    unnamed x12, local copies, waits for them, and re-layouts  11.4 us

commit v1 on v0

--- a/solution.py
+++ b/solution.py
@@ -1,5 +1,7 @@
 import functools
+import itertools
 import math
+import random
 
 import jax
 import jax.numpy as jnp
@@ -36,11 +38,13 @@
     low = [("d", 2)]
     near = [("d", 1)]
     wide = [("f", b) for b in range(nf)]
-    return (low + near + high + wide, high + wide + low + near)
+    first = [(low, near, high, wide), (high, wide, low, near)]
+    rest = [p for p in itertools.permutations((low, near, high, wide)) if p not in first]
+    return [tuple(bit for group in order for bit in group) for order in first + rest]
 
 
 def cut_pieces(shapes):
-    pieces, waves, large = [], [], 0
+    pieces, ranks, large = [], [], 0
     for m, (rows, cols) in enumerate(shapes):
         count = 4 if rows * cols > 40000 else 2
         if rows % (16 * count) == 0:
@@ -54,9 +58,9 @@
         for cut in cuts:
             pieces.append((m, *cut, large % 2))
             small = rows * cols < 2048
-            waves.append(0 if small else large // 4)
+            ranks.append(0 if small else large)
             large += 0 if small else 1
-    return pieces, waves
+    return pieces, ranks
 
 
 class Place:
@@ -102,10 +106,11 @@
         self.arrays = arrays
         self.given = arrays
         self.made = []
+        self.adds = False
         self.nd, self.nf = mesh_bits()
-        orders = hop_orders(self.nd, self.nf)
-        self.cuts, self.waves = cut_pieces([a.shape for a in arrays])
-        self.routes = [tuple(orders[cut[-1]]) + (CORE,) for cut in self.cuts]
+        self.orders = [order + (CORE,) for order in hop_orders(self.nd, self.nf)]
+        self.cuts, self.ranks = cut_pieces([a.shape for a in arrays])
+        self.routes = [self.orders[cut[-1]] for cut in self.cuts]
         self.hops = self.nd + self.nf
         lead = (2,) * self.hops
         self.out_shape = [jax.ShapeDtypeStruct(lead + a.shape, a.dtype) for a in arrays]
@@ -195,13 +200,14 @@
         made = made or {}
         self.given = given
         self.made = list(made)
+        self.adds = True
         arrays = list(given) + list(made.values())
         self.arrays = arrays
         self.nd, self.nf = mesh_bits()
-        orders = hop_orders(self.nd, self.nf)
+        self.orders = [(CORE,) + order[::-1] for order in hop_orders(self.nd, self.nf)]
         self.hops = self.nd + self.nf
-        self.cuts, self.waves = cut_pieces([a.shape[-2:] for a in arrays])
-        self.routes = [(CORE,) + tuple(reversed(orders[cut[-1]])) for cut in self.cuts]
+        self.cuts, self.ranks = cut_pieces([a.shape[-2:] for a in arrays])
+        self.routes = [self.orders[cut[-1]] for cut in self.cuts]
         self.scratch = []
         for m, row, rows, col, cols, _ in self.cuts:
             for h in range(-1 if m < len(self.given) else 0, self.hops):
@@ -292,6 +298,10 @@
 LINK_RATE = 46e3
 CORE_RATE = 380e3
 LATENCY = 2.5
+ENTRY = 3.0
+ISSUE = 0.06
+ADD_RATE = 1800e3
+SEARCH = 1500
 
 
 class Phase:
@@ -300,30 +310,13 @@
         self.needs, self.makes = set(needs), set(makes)
 
 
-def plan_steps(jobs, phases):
-    order = []
-    for j, job in enumerate(jobs):
-        order += sorted(
-            (wave + h, wave, (j, k), h)
-            for k, wave in enumerate(job.waves)
-            for h in range(job.hops + 1)
-        )
-    times, first, after = [], [], {}
-    clock = 0.0
-    for phase in phases:
-        first.append(len(times))
-        for _ in range(phase.steps):
-            times += [clock + mark for mark in phase.marks]
-            clock += phase.marks[-1]
-        for m in phase.makes:
-            after[len(jobs) - 1, m] = len(times)
+def place_steps(order, job, times, clock, limits, after, counted=True):
     total = len(times)
     limit = [total] * len(order)
-    for phase, begin in zip(phases, first):
+    for needs, begin in limits:
         last = -1
-        for i, (_, _, n, h) in enumerate(order):
-            j, k = n
-            if j == 0 and h == jobs[j].hops and jobs[j].cuts[k][0] in phase.needs:
+        for i, (k, h) in enumerate(order):
+            if h == job.hops and job.cuts[k][0] in needs:
                 last = i
         for i in range(last + 1):
             limit[i] = min(limit[i], begin)
@@ -350,28 +343,80 @@
 
     slots = [[] for _ in range(total)]
     tail = []
-    at, late = 0, 0.0
-    for i, (_, _, n, h) in enumerate(order):
-        j, k = n
-        job = jobs[j]
+    at, late, started = 0, ENTRY if counted else 0.0, 0.0
+    for i, (k, h) in enumerate(order):
         ready = now
         if h:
-            advance((n, h - 1), math.inf)
-            ready = max(ready, done[n, h - 1])
+            advance((k, h - 1), math.inf)
+            ready = max(ready, done[k, h - 1])
         else:
-            at = max(at, after.get((j, job.cuts[k][0]), 0))
+            at = max(at, after.get(job.cuts[k][0], 0))
         while at < min(limit[i], total) and times[at] + late < ready - 0.3:
             at += 1
+        spent = ISSUE + (job.sizes(k)[h - 1] / ADD_RATE if h and job.adds else 0.0)
+        spent = spent if counted else 0.0
         if at < total:
-            slots[at].append((n, h))
-            late += max(ready - times[at] - late, 0.0)
-            ready = max(ready, times[at] + late)
+            slots[at].append((k, h))
+            ready = max(ready, times[at] + late) + spent
+            late = ready - times[at]
         else:
-            tail.append((n, h))
+            ready = max(ready, clock + late) + spent
+            tail.append((k, h))
+        started += ready
         advance(None, ready)
         if h < job.hops:
-            waiting.setdefault(job.routes[k][h], []).append([(n, h), float(job.sizes(k)[h])])
-    return slots, tail
+            waiting.setdefault(job.routes[k][h], []).append([(k, h), float(job.sizes(k)[h])])
+    end = max(now, clock + late)
+    return end + 0.2 * max(done.values()) + 0.1 * started / len(order), slots, tail
+
+
+def plan_steps(job, phases, search):
+    times, limits, after = [], [], {}
+    clock = 0.0
+    for phase in phases:
+        limits.append((phase.needs, len(times)))
+        for _ in range(phase.steps):
+            times += [clock + mark for mark in phase.marks]
+            clock += phase.marks[-1]
+        for m in phase.makes:
+            after[m] = len(times)
+    known = (job, times, clock, limits, after)
+
+    def waves(width, lag):
+        order = []
+        for k, rank in enumerate(job.ranks):
+            wave = rank // width + (lag if job.cuts[k][0] in after else 0)
+            order += [(wave + h, wave, k, h) for h in range(job.hops + 1)]
+        return [(k, h) for _, _, k, h in sorted(order)]
+
+    if not search:
+        return place_steps(waves(4, 0), *known, False)[1:]
+    lags = range(4) if after else (0,)
+    starts = [waves(width, lag) for width in (3, 4, 5, 6) for lag in lags]
+    best, order = min((place_steps(start, *known)[0], start) for start in starts)
+    draw = random.Random(1)
+    for _ in range(search):
+        if draw.random() < 0.3:
+            k = draw.randrange(len(job.cuts))
+            kept = job.routes[k]
+            job.routes[k] = draw.choice(job.orders)
+            cost = place_steps(order, *known)[0]
+            if cost < best:
+                best = cost
+            else:
+                job.routes[k] = kept
+            continue
+        i = draw.randrange(len(order))
+        k, h = order[i]
+        low_end = order.index((k, h - 1)) + 1 if h else 0
+        high_end = order.index((k, h + 1)) - 1 if h < job.hops else len(order) - 1
+        j = draw.randint(max(low_end, i - 12), max(low_end, min(high_end, i + 12)))
+        moved = list(order)
+        moved.insert(j, moved.pop(i))
+        cost = place_steps(moved, *known)[0]
+        if cost < best:
+            best, order = cost, moved
+    return place_steps(order, *known)[1:]
 
 
 class Names:
@@ -380,32 +425,26 @@
             setattr(self, name, ref)
 
 
-def carrying_kernel(phases, jobs, plan, names, *refs):
+def carrying_kernel(phases, job, plan, names, *refs):
     spans, start = [], 0
     for count in [len(group) for group in names]:
         spans.append(refs[start : start + count])
         start += count
-    given, landed, worked = [], [], []
-    for kind, parts in ((given, 1), (landed, 3), (worked, 5)):
-        rest = list(spans[parts])
-        for job in jobs:
-            count = (len(job.given), len(job.out_shape), len(job.scratch))[parts // 2]
-            kind.append([rest.pop(0) for _ in range(count)])
-    r = Names(names[0] + names[2] + names[4], spans[0] + spans[2] + spans[4])
+    own_in, job_in, own_out, job_out, own_scratch, job_scratch = spans
+    r = Names(names[0] + names[2] + names[4], own_in + own_out + own_scratch)
     now = pl.program_id(0)
     slots, tail = plan
-    place = Place(jobs[0].nd, jobs[0].nf)
-    r.gathered = landed[0]
-    for job, ins, outs, scratch in zip(jobs, given, landed, worked):
-        job.bind(place, ins + [getattr(r, name) for name in job.made], outs, scratch)
+    place = Place(job.nd, job.nf)
+    r.gathered = job_out
+    made = [getattr(r, name) for name in job.made]
+    job.bind(place, list(job_in) + made, job_out, job_scratch)
 
     def run(items, opening=False):
         if opening:
-            for job in jobs:
-                job.start()
+            job.start()
             place.barrier()
-        for (j, k), h in items:
-            jobs[j].step(k, h)
+        for k, h in items:
+            job.step(k, h)
 
     base, begin = 0, 0
     for phase in phases:
@@ -433,11 +472,9 @@
         pl.when(now == begin - 1)(functools.partial(run, tail))
 
 
-def carry(phases, ins, outs, scratch, jobs, ident):
-    plan = plan_steps(jobs, phases)
-    given = [array for job in jobs for array in job.given]
-    landed = [shape for job in jobs for shape in job.out_shape]
-    worked = [item for job in jobs for item in job.scratch]
+def carry(phases, ins, outs, scratch, job, ident, search=0):
+    plan = plan_steps(job, phases, search)
+    given, landed, worked = list(job.given), list(job.out_shape), list(job.scratch)
     names = (
         list(ins),
         [None] * len(given),
@@ -447,11 +484,10 @@
         [None] * len(worked),
     )
     results = pl.pallas_call(
-        functools.partial(carrying_kernel, phases, jobs, plan, names),
+        functools.partial(carrying_kernel, phases, job, plan, names),
         grid=(sum(phase.steps for phase in phases),),
         in_specs=[spec for _, spec in ins.values()] + [ANYWHERE] * len(given),
-        out_specs=[spec for _, spec in outs.values()]
-        + [spec for job in jobs for spec in job.out_specs],
+        out_specs=[spec for _, spec in outs.values()] + list(job.out_specs),
         out_shape=[shape for shape, _ in outs.values()] + landed,
         scratch_shapes=list(scratch.values()) + worked,
         compiler_params=pltpu.CompilerParams(
@@ -459,9 +495,7 @@
         ),
     )(*[array for array, _ in ins.values()], *given)
     r = Names(list(outs), results)
-    r.landed, rest = [], list(results[len(outs) :])
-    for job in jobs:
-        r.landed.append([rest.pop(0) for _ in job.out_shape])
+    r.landed = results[len(outs) :]
     return r
 
 
@@ -1038,8 +1072,8 @@
         begin.append(begin[-1] + count)
         return begin[-2]
 
-    phase(project_keys_phase, steps, (0.0, 1.4), needs=range(3))
-    phase(attend_image_phase, steps, (0.0, 1.9, 3.8))
+    phase(project_keys_phase, steps, (0.0, 1.7), needs=range(3))
+    phase(attend_image_phase, steps, (0.0, 0.9, 1.8))
     stages = 1 << nf
     marks = [0.0, 1.1] + [1.1 + 1.0 * (k + 1) / stages for k in range(stages)]
     marks += [3.3, 4.4, 5.7, 6.4]
@@ -1047,9 +1081,9 @@
         functools.partial(image_phase, width_text, norm_wide), 2, marks, needs=range(3, 7)
     )
     at_image_grads = phase(image_grads_phase, 4, (0.0, 1.0))
-    at_back = phase(back_image_phase, steps, (0.0, 2.3, 4.6))
-    at_grads = phase(key_grads_phase, 2, (0.0, 4.2))
-    at_attend = phase(attend_text_phase, steps, (0.0, 0.8, 2.8, 4.8), needs=range(7, 10))
+    at_back = phase(back_image_phase, steps, (0.0, 0.8, 1.7))
+    at_grads = phase(key_grads_phase, 2, (0.0, 2.4))
+    at_attend = phase(attend_text_phase, steps, (0.0, 0.8, 1.7, 2.6), needs=range(7, 10))
     third = width_text // 3
 
     def grad_out(weight_shard, inner, first, count, size):
@@ -1130,10 +1164,11 @@
             diq_sum=pltpu.VMEM(image_shape, f32),
             cot_wide=vmem(block_i, width_image, f32),
         ),
-        [gather],
+        gather,
         0,
+        SEARCH,
     )
-    whole = [whole_weight(s, g) for s, g in zip(gather.given, a.landed[0]) if s is not norm_params]
+    whole = [whole_weight(s, g) for s, g in zip(gather.given, a.landed) if s is not norm_params]
     w_tk, w_tv, w_iq, _, _, _, w_tq, w_ik, w_iv, w_to, w_ti, w_tu = whole
 
     job = Reduce(
@@ -1192,10 +1227,10 @@
             ffn=vmem(rows_text, width_text),
             branch=vmem(rows_text, width_text),
         ),
-        [job],
+        job,
         1,
     )
-    o_io, o_ii, o_iu, o_iq, o_tk, o_tv = b.landed[0]
+    o_io, o_ii, o_iu, o_iq, o_tk, o_tv = b.landed
 
     norm_rows = norm_blocks(jnp.concatenate([b.text_ngrad, a.image_ngrad], axis=1))
     job = Reduce(
@@ -1212,8 +1247,8 @@
         ),
     )
     phases, begin = [], [0]
-    at_back = phase(back_text_phase, steps, (0.0, 2.3, 4.6))
-    phase(query_grads_phase, 2, (0.0, 3.2), makes=range(4, 7))
+    at_back = phase(back_text_phase, steps, (0.0, 0.8, 1.7))
+    phase(query_grads_phase, 2, (0.0, 2.0), makes=range(4, 7))
     at_data = phase(data_grads_phase, steps, (0.0, 0.9, 1.8, 2.6))
     probs = during(at_back, steps, (n * heads, padded, length))
     back_rows = during(at_back, steps, (n * length, wide))
@@ -1256,10 +1291,11 @@
             g_ik=pltpu.VMEM(lead + image_key.shape, bf),
             g_iv=pltpu.VMEM(lead + image_value.shape, bf),
         ),
-        [job],
+        job,
         2,
+        SEARCH,
     )
-    o_tu, o_ti, o_to, o_norm, o_tq, o_ik, o_iv = c.landed[0]
+    o_tu, o_ti, o_to, o_norm, o_tq, o_ik, o_iv = c.landed
     owned = pass_on([o_iq, o_ik, o_iv, o_tq, o_tk, o_tv, o_io, o_to, o_ii, o_iu, o_ti, o_tu])
     return (
         b.text_out,

time: 331 us -> 321 us (0.970)
  Pallas kernels: 314 us -> 304 us
    pallas_call x3, Pallas kernels: 311 us -> 301 us  [carry(): pl.pallas_call(functools.partial(carrying_kernel, phases, job, plan, name...]
where the time goes in v1:
time: 321 us; the launch traced here: 320 us
  Pallas kernels  304 us (95%)
  local copies, waits for them, and re-layouts  13.5 us (4%)
    pallas_call x3, Pallas kernels, carry(): pl.pallas_call(functools.partial(carrying_kernel, phases, job, plan, name...  301 us
    unnamed x12, local copies, waits for them, and re-layouts  11.4 us

profile of v1, /device:TPU:0, one launch (start us, length us, event | category | flops | bytes accessed | tf_op | source)
XLA Modules:
  0.0 320.3 jit_solution(3896731291138729556)
XLA Ops:
  0.7 1.2 broadcast_subtract_fusion.refs_1_.refs_0_
  1.8 1.6 copy.37.refs_4_
  3.4 2.2 copy.38.refs_5_
  5.7 136.2 %shard_map.323 = (bf16[2,48,1024]{2,1,0:T(8,128)(2,1)}, bf16[2,48,1024]{2,1,0:T(8,128)(2,1)}, bf16[1024,1024]{1,0:T(8,128)(2,1)}, f32[64,48,128]{2,1,0:T(8,128)}...) custom-call(s32[8]{0:T(128)} %refs_0_.3, ...), custom_call_target="tpu_custom_call" | custom-call | tf_op jit(solution)/shard_map/pallas_call | solution.py:486
  141.8 0.0 copy-start.2
  141.8 81.4 %shard_map.324 = (bf16[8,128,768]{2,1,0:T(8,128)(2,1)}, f32[1024,768]{1,0:T(8,128)}, bf16[1024,1024]{1,0:T(8,128)(2,1)}, f32[4,768]{1,0:T(4,128)}, bf16[2,3072,3...) custom-call(s32[8]{0:T(128)} %refs_0_.3, ...), custom_call_target="tpu_custom_call" | custom-call | tf_op jit(solution)/shard_map/pallas_call | solution.py:486
  223.3 0.0 copy-done.2
  223.3 0.7 pad_maximum_fusion
  224.0 0.2 reshape.119
  224.2 0.7 pad.4
  224.9 0.0 copy-start.1
  224.9 83.9 %shard_map.325 = (f32[1024,768]{1,0:T(8,128)}, f32[2,36,1024]{2,1,0:T(8,128)}, f32[192,384]{1,0:T(8,128)}, f32[48,1536]{1,0:T(8,128)}, f32[64,384]{1,0:T(8,128)}...) custom-call(s32[8]{0:T(128)} %broadcast_subtract_fusion.refs_1_.refs_0_, ...), custom_call_target="tpu_custom_call" | custom-call | tf_op jit(solution)/shard_map/pallas_call | solution.py:486
  308.8 1.3 slice.3
  310.0 1.9 copy.41
  311.9 0.0 copy-done.1
  311.9 1.1 copy.40
  313.1 2.7 shard_map.326
  315.8 0.0 copy-start
  315.8 2.8 copy.46
  318.6 0.0 copy-done
  318.6 1.7 copy.47
  (1 shorter events, 0.0 us)
Async XLA Ops:
  141.8 81.4 %copy-start.2 = (f32[4,1024]{1,0:T(4,128)S(1)}, f32[4,1024]{1,0:T(4,128)}, u32[]{:S(2)}) copy-start(f32[4,1024]{1,0:T(4,128)} %get-tuple-element.113) | copy-start | bytes 49156
  224.9 87.1 %copy-start.1 = (bf16[8,36,1024]{2,1,0:T(8,128)(2,1)S(1)}, bf16[8,36,1024]{2,1,0:T(8,128)(2,1)}, u32[]{:S(2)}) copy-start(bf16[8,36,1024]{2,1,0:T(8,128)(2,1)} %get-tuple-element.142) | copy-start | bytes 1769476
  315.8 2.8 copy-start

commit v2 on v1

--- a/solution.py
+++ b/solution.py
@@ -297,7 +297,7 @@
 
 LINK_RATE = 46e3
 CORE_RATE = 380e3
-LATENCY = 2.5
+LATENCY = 3.2
 ENTRY = 3.0
 ISSUE = 0.06
 ADD_RATE = 1800e3
@@ -565,6 +565,33 @@
         copy.wait()
 
 
+def coming(r, names):
+    return [
+        pltpu.make_async_copy(getattr(r, "far_" + name), getattr(r, name), r.sems.at[n])
+        for n, name in names
+    ]
+
+
+def start_all(copies):
+    for copy in copies:
+        copy.start()
+
+
+def wait_all(copies):
+    for copy in copies:
+        copy.wait()
+
+
+def at_first(step, act, copies):
+    pl.when(step == 0)(functools.partial(act, copies))
+
+
+TEXT_FAR = ((0, "w_ti"), (1, "w_tu"))
+LAST_FAR = tuple(
+    enumerate(("text", "image_dz", "w_iq", "w_ik", "w_iv", "w_tq", "w_tk", "w_tv"))
+)
+
+
 ROW_PAIRS = 2
 
 
@@ -685,7 +712,7 @@
         tick()
 
 
-def stream_rows(r, step, tick, limits, x, ctx, cot, norms, weights, keeps, outs):
+def stream_rows(r, step, tick, limits, x, ctx, cot, norms, weights, keeps, outs, waits=()):
     w_out, w_inner, w_outer = weights
     mid_ref, act_ref, hid_ref, ffn_ref, branch_ref = keeps
     out, dz_out, dctx_out, ngrad = outs
@@ -722,12 +749,16 @@
     mid_ref[...] = mid_low
     tick()
     cols = w_inner.shape[2]
+    if waits:
+        at_first(step, wait_all, waits[:1])
     for f in range(w_inner.shape[0]):
         at = slice(f * cols, (f + 1) * cols)
         act, grad = gelu_pair(dot_nn(mid_low, w_inner[f]))
         act_ref[:, at] = low(act)
         hid_ref[:, at] = low(grad)
         tick()
+    if waits:
+        at_first(step, wait_all, waits[1:])
     second_hat, second_inv = normalize(mid + times(act_ref[...], w_outer))
     result = low((second_hat * norms[2] + norms[3]) * kept)
     for q in range(group):
@@ -874,6 +905,8 @@
 
 def text_phase(r, step, tick):
     tick()
+    copies = coming(r, TEXT_FAR)
+    at_first(step, start_all, copies)
     rows = r.x.shape[0]
     here = rows_at(step, rows)
     norms = [r.norms[n : n + 1, : r.x.shape[1]] for n in range(4)]
@@ -889,6 +922,7 @@
         (r.w_to, r.w_ti, r.w_tu),
         [ref.at[here] for ref in (r.mid, r.act, r.hid, r.ffn, r.branch)],
         (r.text_out, r.text_dz, r.dctx, r.text_ngrad),
+        copies,
     )
 
 
@@ -902,6 +936,7 @@
 
 def back_text_phase(r, step, tick):
     tick()
+    at_first(step, start_all, coming(r, LAST_FAR))
     regions, length = r.tprob.shape[1:]
     heads = r.tq.shape[1] // HDIM
     columns = [slice(h * HDIM, (h + 1) * HDIM) for h in range(heads)]
@@ -938,6 +973,7 @@
 
 def query_grads_phase(r, step, tick):
     tick()
+    at_first(step, wait_all, coming(r, LAST_FAR[:1]))
     here = rows_at(step, r.text.shape[1] // 2)
     put_half(r.g_tq, step, r.text[:, here], r.dtq[...])
     dik, div = low(r.dik_sum[...]), low(r.div_sum[...])
@@ -955,6 +991,7 @@
     pairs = r.owner.shape[0]
     slots = r.image_dz.shape[0] // pairs
     tick()
+    at_first(step, wait_all, coming(r, LAST_FAR[1:]))
 
     @pl.when(step == 0)
     def _():
@@ -1208,8 +1245,8 @@
             cot=(cot_text, by_pair),
             norms=resident(a.norms),
             w_to=resident(w_to),
-            w_ti=resident(w_ti),
-            w_tu=resident(w_tu),
+            far_w_ti=(w_ti, ANYWHERE),
+            far_w_tu=(w_tu, ANYWHERE),
         ),
         dict(
             text_out=(struct(cot_text.shape, bf), by_pair),
@@ -1221,6 +1258,9 @@
             g_to=grad_out(text_output, wide, at_to, 4, wide // 4),
         ),
         dict(
+            w_ti=pltpu.VMEM(w_ti.shape, bf),
+            w_tu=pltpu.VMEM(w_tu.shape, bf),
+            sems=pltpu.SemaphoreType.DMA((len(TEXT_FAR),)),
             mid=vmem(rows_text, width_text),
             act=vmem(rows_text, inner),
             hid=vmem(rows_text, inner),
@@ -1263,25 +1303,34 @@
             tq=(a.tq, back_rows),
             tprob=(a.tprob, probs),
             dtc=(b.dctx, back_rows),
-            text=resident(text),
+            far_text=(text, ANYWHERE),
             image=resident(a.image_rows),
             text_dz=(b.text_dz, data_out),
             dtk=(a.dtk, data_rows),
             dtv=(a.dtv, data_rows),
-            image_dz=resident(a.image_dz),
+            far_image_dz=(a.image_dz, ANYWHERE),
             diq=resident(a.diq),
-            w_tq=resident(w_tq),
-            w_tk=resident(w_tk),
-            w_tv=resident(w_tv),
-            w_iq=resident(w_iq),
-            w_ik=resident(w_ik),
-            w_iv=resident(w_iv),
+            far_w_tq=(w_tq, ANYWHERE),
+            far_w_tk=(w_tk, ANYWHERE),
+            far_w_tv=(w_tv, ANYWHERE),
+            far_w_iq=(w_iq, ANYWHERE),
+            far_w_ik=(w_ik, ANYWHERE),
+            far_w_iv=(w_iv, ANYWHERE),
         ),
         dict(
             text_grad=(struct((rows_text, width_text), f32), data_out),
             image_grad=(struct(image_states.shape, f32), fixed(image_states.shape)),
         ),
         dict(
+            text=vmem(rows_text, width_text),
+            image_dz=vmem(rows_image, width_image, f32),
+            w_tq=pltpu.VMEM(w_tq.shape, bf),
+            w_tk=pltpu.VMEM(w_tk.shape, bf),
+            w_tv=pltpu.VMEM(w_tv.shape, bf),
+            w_iq=pltpu.VMEM(w_iq.shape, bf),
+            w_ik=pltpu.VMEM(w_ik.shape, bf),
+            w_iv=pltpu.VMEM(w_iv.shape, bf),
+            sems=pltpu.SemaphoreType.DMA((len(LAST_FAR),)),
             dtq=vmem(rows_text, wide),
             dik=pltpu.VMEM(image_shape, bf),
             div=pltpu.VMEM(image_shape, bf),

time: 321 us -> 312 us (0.972)
  Pallas kernels: 304 us -> 296 us
    pallas_call x3, Pallas kernels: 301 us -> 293 us  [carry(): pl.pallas_call(functools.partial(carrying_kernel, phases, job, plan, name...]
where the time goes in v2:
time: 312 us
  Pallas kernels  296 us (95%)
  local copies, waits for them, and re-layouts  13.5 us (4%)
    pallas_call x3, Pallas kernels, carry(): pl.pallas_call(functools.partial(carrying_kernel, phases, job, plan, name...  293 us
    unnamed x12, local copies, waits for them, and re-layouts  11.4 us

profile of v2, /device:TPU:0, one launch (start us, length us, event | category | flops | bytes accessed | tf_op | source)
XLA Modules:
  0.0 311.7 jit_solution(4061498325431721415)
XLA Ops:
  0.7 1.2 broadcast_subtract_fusion.refs_1_.refs_0_
  1.8 1.6 copy.37.refs_4_
  3.4 2.2 copy.38.refs_5_
  5.7 134.2 %shard_map.323 = (bf16[2,48,1024]{2,1,0:T(8,128)(2,1)}, bf16[2,48,1024]{2,1,0:T(8,128)(2,1)}, bf16[1024,1024]{1,0:T(8,128)(2,1)}, f32[64,48,128]{2,1,0:T(8,128)}...) custom-call(s32[8]{0:T(128)} %refs_0_.3, ...), custom_call_target="tpu_custom_call" | custom-call | tf_op jit(solution)/shard_map/pallas_call | solution.py:486
  139.9 0.0 copy-start.2
  139.9 77.8 %shard_map.324 = (bf16[8,128,768]{2,1,0:T(8,128)(2,1)}, f32[1024,768]{1,0:T(8,128)}, bf16[1024,1024]{1,0:T(8,128)(2,1)}, f32[4,768]{1,0:T(4,128)}, bf16[2,3072,3...) custom-call(s32[8]{0:T(128)} %refs_0_.3, ...), custom_call_target="tpu_custom_call" | custom-call | tf_op jit(solution)/shard_map/pallas_call | solution.py:486
  217.7 0.0 copy-done.2
  217.7 0.7 pad_maximum_fusion
  218.5 0.2 reshape.119
  218.7 0.7 pad.4
  219.3 0.0 copy-start.1
  219.3 80.8 %shard_map.325 = (f32[1024,768]{1,0:T(8,128)}, f32[2,36,1024]{2,1,0:T(8,128)}, f32[192,384]{1,0:T(8,128)}, f32[48,1536]{1,0:T(8,128)}, f32[64,384]{1,0:T(8,128)}...) custom-call(s32[8]{0:T(128)} %broadcast_subtract_fusion.refs_1_.refs_0_, ...), custom_call_target="tpu_custom_call" | custom-call | tf_op jit(solution)/shard_map/pallas_call | solution.py:486
  300.1 1.3 slice.3
  301.4 1.9 copy.41
  303.3 0.0 copy-done.1
  303.3 1.1 copy.40
  304.5 2.7 shard_map.326
  307.2 0.0 copy-start
  307.2 2.8 copy.46
  310.0 0.0 copy-done
  310.0 1.7 copy.47
  (1 shorter events, 0.0 us)
Async XLA Ops:
  139.9 77.8 %copy-start.2 = (f32[4,1024]{1,0:T(4,128)S(1)}, f32[4,1024]{1,0:T(4,128)}, u32[]{:S(2)}) copy-start(f32[4,1024]{1,0:T(4,128)} %get-tuple-element.113) | copy-start | bytes 49156
  219.3 84.0 %copy-start.1 = (bf16[8,36,1024]{2,1,0:T(8,128)(2,1)S(1)}, bf16[8,36,1024]{2,1,0:T(8,128)(2,1)}, u32[]{:S(2)}) copy-start(bf16[8,36,1024]{2,1,0:T(8,128)(2,1)} %get-tuple-element.142) | copy-start | bytes 1769476
  307.2 2.8 copy-start

commit v3 on v2

--- a/solution.py
+++ b/solution.py
@@ -394,7 +394,7 @@
     lags = range(4) if after else (0,)
     starts = [waves(width, lag) for width in (3, 4, 5, 6) for lag in lags]
     best, order = min((place_steps(start, *known)[0], start) for start in starts)
-    draw = random.Random(1)
+    draw = random.Random(1 if job.adds else 7)
     for _ in range(search):
         if draw.random() < 0.3:
             k = draw.randrange(len(job.cuts))

time: 312 us -> 309 us (level)
  no operation moved by 1% of the time
where the time goes in v3:
time: 309 us
  Pallas kernels  293 us (95%)
  local copies, waits for them, and re-layouts  13.5 us (4%)
    pallas_call x3, Pallas kernels, carry(): pl.pallas_call(functools.partial(carrying_kernel, phases, job, plan, name...  290 us
    unnamed x12, local copies, waits for them, and re-layouts  11.4 us

profile of v3, /device:TPU:0, one launch (start us, length us, event | category | flops | bytes accessed | tf_op | source)
XLA Modules:
  0.0 309.1 jit_solution(10445705578986171956)
XLA Ops:
  0.7 1.2 broadcast_subtract_fusion.refs_1_.refs_0_
  1.8 1.6 copy.37.refs_4_
  3.4 2.2 copy.38.refs_5_
  5.7 130.5 %shard_map.323 = (bf16[2,48,1024]{2,1,0:T(8,128)(2,1)}, bf16[2,48,1024]{2,1,0:T(8,128)(2,1)}, bf16[1024,1024]{1,0:T(8,128)(2,1)}, f32[64,48,128]{2,1,0:T(8,128)}...) custom-call(s32[8]{0:T(128)} %refs_0_.3, ...), custom_call_target="tpu_custom_call" | custom-call | tf_op jit(solution)/shard_map/pallas_call | solution.py:486
  136.2 0.0 copy-start.2
  136.2 78.2 %shard_map.324 = (bf16[8,128,768]{2,1,0:T(8,128)(2,1)}, f32[1024,768]{1,0:T(8,128)}, bf16[1024,1024]{1,0:T(8,128)(2,1)}, f32[4,768]{1,0:T(4,128)}, bf16[2,3072,3...) custom-call(s32[8]{0:T(128)} %refs_0_.3, ...), custom_call_target="tpu_custom_call" | custom-call | tf_op jit(solution)/shard_map/pallas_call | solution.py:486
  214.4 0.0 copy-done.2
  214.4 0.7 pad_maximum_fusion
  215.1 0.2 reshape.119
  215.4 0.7 pad.4
  216.0 0.0 copy-start.1
  216.0 81.6 %shard_map.325 = (f32[1024,768]{1,0:T(8,128)}, f32[2,36,1024]{2,1,0:T(8,128)}, f32[192,384]{1,0:T(8,128)}, f32[48,1536]{1,0:T(8,128)}, f32[64,384]{1,0:T(8,128)}...) custom-call(s32[8]{0:T(128)} %broadcast_subtract_fusion.refs_1_.refs_0_, ...), custom_call_target="tpu_custom_call" | custom-call | tf_op jit(solution)/shard_map/pallas_call | solution.py:486
  297.6 1.3 slice.3
  298.9 1.9 copy.41
  300.8 0.0 copy-done.1
  300.8 1.1 copy.40
  301.9 2.7 shard_map.326
  304.6 0.0 copy-start
  304.7 2.8 copy.46
  307.5 0.0 copy-done
  307.5 1.7 copy.47
  (1 shorter events, 0.0 us)
Async XLA Ops:
  136.2 78.3 %copy-start.2 = (f32[4,1024]{1,0:T(4,128)S(1)}, f32[4,1024]{1,0:T(4,128)}, u32[]{:S(2)}) copy-start(f32[4,1024]{1,0:T(4,128)} %get-tuple-element.113) | copy-start | bytes 49156
  216.0 84.8 %copy-start.1 = (bf16[8,36,1024]{2,1,0:T(8,128)(2,1)S(1)}, bf16[8,36,1024]{2,1,0:T(8,128)(2,1)}, u32[]{:S(2)}) copy-start(bf16[8,36,1024]{2,1,0:T(8,128)(2,1)} %get-tuple-element.142) | copy-start | bytes 1769476
  304.6 2.8 copy-start
